TPU v7x, 32 devices: a whole 2x2x4 slice. The times are simulated.
32 devices in a mesh: groups: 2 (over x), fsdp: 2 (over core), rows: 8 (over z, y).
Axes of the slice: x: 2, y: 2, z: 4, core: 2. Of those that a mesh axis runs over, the one named last changes fastest.
Arguments:
- tokens: bfloat16 [4, 128, 16, 1024], P(('groups', 'fsdp'), 'rows'), parts along dimension 0, may hold values from -6 to 6
- cell_mask: int32 [4, 128, 16], P(('groups', 'fsdp'), 'rows'), parts along dimension 0, may hold values 0 or 1
- shifts: int32 [2], replicated, may hold values from 1 to 15
- projection_in: bfloat16 [1024, 1536], P(('fsdp', 'rows')), may hold values from -2 to 2
- projection_out: bfloat16 [512, 1024], P(('fsdp', 'rows')), may hold values from -0.25 to 0.25
- cotangent: bfloat16 [4, 128, 16, 1024], P(('groups', 'fsdp'), 'rows'), parts along dimension 0, may hold values from -6 to 6
Outputs:
- output: bfloat16 [4, 128, 16, 1024], P(('groups', 'fsdp'), 'rows'), parts along dimension 0
- grad_tokens: bfloat16 [4, 128, 16, 1024], P(('groups', 'fsdp'), 'rows'), parts along dimension 0
- projection_in_grad: float32 [2048, 1536], P(('groups', 'fsdp', 'rows')), parts along dimension 0
- projection_out_grad: float32 [1024, 1024], P(('groups', 'fsdp', 'rows')), parts along dimension 0
There are 2 independent parts, one for each index of `groups`. A program takes and returns all parts, laid end to end along the dimension named above; an argument that names none is the same for every part. Nothing has to cross between parts.
All inputs are finite; a program needn't handle non-finite values. No bound on the sum of `cell_mask` on one device may be relied on, other than what follows from the above.
Results may differ from a plain program's by a relative error of at most 0.011.
Values may be sent and summed in bfloat16 or wider, within the bound.
No kernel may reach another device: no remote copies, remote signals or barrier semaphores. Data moves between devices by JAX's collectives and lax.ppermute only.
A program may use at most 64 MiB of HBM per device.

v0:
```python
import jax
import jax.numpy as jnp
from jax import lax
from jax.sharding import PartitionSpec as P

HEADS = 8
HD = 64
WIN = 16


def shifted(block, axis, distance):
    devices = range(lax.axis_size(axis))
    route = [((i - distance) % len(devices), i) for i in devices]
    return lax.ppermute(block, axis, route)


def roll_columns(grid_field, offset):
    col_count = grid_field.shape[1]
    doubled = jnp.concatenate([grid_field, grid_field], axis=1)
    return lax.dynamic_slice_in_dim(doubled, offset, col_count, 1)


def into_windows(grid_field):
    row_count, col_count, channels = grid_field.shape
    blocks = grid_field.reshape(row_count // WIN, WIN, col_count // WIN, WIN, channels)
    return blocks.transpose(0, 2, 1, 3, 4).reshape(-1, WIN * WIN, channels)


def from_windows(windowed, row_count, col_count):
    channels = windowed.shape[-1]
    blocks = windowed.reshape(row_count // WIN, col_count // WIN, WIN, WIN, channels)
    return blocks.transpose(0, 2, 1, 3, 4).reshape(row_count, col_count, channels)


def normalize(values_f32):
    mean_value = jnp.mean(values_f32, axis=-1, keepdims=True)
    centered = values_f32 - mean_value
    variance = jnp.mean(centered * centered, axis=-1, keepdims=True)
    inv_std = lax.rsqrt(variance + 1e-05)
    return (centered * inv_std, inv_std)


def body(tokens, cell_mask, shifts, projection_in, projection_out, cotangent):
    row_count = tokens.shape[1]
    col_count = tokens.shape[2]
    model_dim = tokens.shape[3]
    hidden_width = HEADS * HD
    score_scale = HD ** (-0.5)
    grid_rows = row_count * lax.axis_size("rows")
    shift_row = shifts[0]
    shift_col = shifts[1]
    full_in, full_out = (
        lax.all_gather(projection_in, ("fsdp", "rows"), axis=0, tiled=True),
        lax.all_gather(projection_out, ("fsdp", "rows"), axis=0, tiled=True),
    )
    mask_wire = cell_mask.astype(jnp.bfloat16)
    next_tokens, next_mask = shifted((tokens, mask_wire), "rows", -1)

    def to_slab(own_rows, next_rows):
        joined = jnp.concatenate([own_rows[0], next_rows[0]], axis=0)
        return roll_columns(lax.dynamic_slice_in_dim(joined, shift_row, row_count, 0), shift_col)

    def to_owner(slab_rows, prev_rows):
        joined = jnp.concatenate([prev_rows, slab_rows], axis=0)
        return lax.dynamic_slice_in_dim(joined, row_count - shift_row, row_count, 0)

    slab_tokens = to_slab(tokens, next_tokens)
    slab_mask = to_slab(mask_wire, next_mask)
    row_ids = (
        lax.axis_index("rows") * row_count + shift_row + jnp.arange(row_count, dtype=jnp.int32)
    ) % grid_rows
    col_ids = (jnp.arange(col_count, dtype=jnp.int32) + shift_col) % col_count
    region = (row_ids < shift_row).astype(jnp.int32)[:, None] * 2 + (col_ids < shift_col).astype(
        jnp.int32
    )[None, :]
    region_win = into_windows(region[:, :, None])[:, :, 0]
    mask_win = into_windows(slab_mask[:, :, None])[:, :, 0] > 0
    token_win = into_windows(slab_tokens)
    window_count = token_win.shape[0]
    window_len = token_win.shape[1]
    allowed = (region_win[:, :, None] == region_win[:, None, :]) & (
        mask_win[:, None, :] | jnp.eye(window_len, dtype=bool)[None]
    )
    normed, inv_std = normalize(token_win.astype(jnp.float32))
    normed_bf = normed.astype(jnp.bfloat16)
    flat_normed = normed_bf.reshape(-1, model_dim)
    packed_heads = jnp.dot(flat_normed, full_in, preferred_element_type=jnp.float32).astype(
        jnp.bfloat16
    )
    packed_heads = packed_heads.reshape(window_count, window_len, 3, HEADS, HD)
    query_heads = packed_heads[:, :, 0]
    key_heads = packed_heads[:, :, 1]
    value_heads = packed_heads[:, :, 2]
    scores = (
        jnp.einsum("wqhd,wkhd->whqk", query_heads, key_heads, preferred_element_type=jnp.float32)
        * score_scale
    )
    scores = jnp.where(allowed[:, None], scores, -1e30)
    row_peak = jnp.max(scores, axis=-1, keepdims=True)
    exp_terms = jnp.exp(scores - row_peak)
    attention = exp_terms / jnp.sum(exp_terms, axis=-1, keepdims=True)
    attention_bf = attention.astype(jnp.bfloat16)
    context = jnp.einsum(
        "whqk,wkhd->wqhd", attention_bf, value_heads, preferred_element_type=jnp.float32
    ).astype(jnp.bfloat16)
    context = context.reshape(window_count, window_len, hidden_width)
    slab_context = roll_columns(from_windows(context, row_count, col_count), col_count - shift_col)
    prev_context = shifted(slab_context, "rows", 1)
    own_context = to_owner(slab_context, prev_context)
    projected = jnp.dot(
        own_context.reshape(-1, hidden_width), full_out, preferred_element_type=jnp.float32
    )
    output = (
        tokens[0].astype(jnp.float32) + projected.reshape(row_count, col_count, model_dim)
    ).astype(jnp.bfloat16)
    next_cotangent = shifted(cotangent, "rows", -1)
    cot_win = into_windows(to_slab(cotangent, next_cotangent))
    flat_cot = cot_win.reshape(-1, model_dim)
    flat_context = context.reshape(-1, hidden_width)
    grad_context = lax.dot_general(
        flat_cot, full_out, (((1,), (1,)), ((), ())), preferred_element_type=jnp.float32
    ).astype(jnp.bfloat16)
    term_out = lax.dot_general(
        flat_context, flat_cot, (((0,), (0,)), ((), ())), preferred_element_type=jnp.float32
    )
    grad_heads = grad_context.reshape(window_count, window_len, HEADS, HD)
    grad_attention = jnp.einsum(
        "wqhd,wkhd->whqk", grad_heads, value_heads, preferred_element_type=jnp.float32
    )
    grad_scores = (
        attention
        * (grad_attention - jnp.sum(grad_attention * attention, axis=-1, keepdims=True))
        * score_scale
    ).astype(jnp.bfloat16)
    grad_query = jnp.einsum(
        "whqk,wkhd->wqhd", grad_scores, key_heads, preferred_element_type=jnp.float32
    )
    grad_key = jnp.einsum(
        "whqk,wqhd->wkhd", grad_scores, query_heads, preferred_element_type=jnp.float32
    )
    grad_value = jnp.einsum(
        "whqk,wqhd->wkhd", attention_bf, grad_heads, preferred_element_type=jnp.float32
    )
    grad_packed = (
        jnp.stack([grad_query, grad_key, grad_value], axis=2)
        .astype(jnp.bfloat16)
        .reshape(-1, 3 * hidden_width)
    )
    term_in = lax.dot_general(
        flat_normed, grad_packed, (((0,), (0,)), ((), ())), preferred_element_type=jnp.float32
    )
    grad_normed = lax.dot_general(
        grad_packed, full_in, (((1,), (1,)), ((), ())), preferred_element_type=jnp.float32
    )
    grad_normed = grad_normed.reshape(window_count, window_len, model_dim)
    grad_win = (
        cot_win.astype(jnp.float32)
        + inv_std
        * (
            grad_normed
            - jnp.mean(grad_normed, axis=-1, keepdims=True)
            - normed * jnp.mean(grad_normed * normed, axis=-1, keepdims=True)
        )
    ).astype(jnp.bfloat16)
    slab_grad = roll_columns(from_windows(grad_win, row_count, col_count), col_count - shift_col)
    prev_grad = shifted(slab_grad, "rows", 1)
    own_grad = to_owner(slab_grad, prev_grad)
    grad_in, grad_out = (
        lax.psum_scatter(term_in, ("fsdp", "rows"), scatter_dimension=0, tiled=True),
        lax.psum_scatter(term_out, ("fsdp", "rows"), scatter_dimension=0, tiled=True),
    )
    return (output[None], own_grad[None], grad_in, grad_out)


def solution(mesh):
    placed = (
        P(("groups", "fsdp"), "rows", None, None),
        P(("groups", "fsdp"), "rows", None),
        P(),
        P(("fsdp", "rows"), None),
        P(("fsdp", "rows"), None),
        P(("groups", "fsdp"), "rows", None, None),
    )
    return jax.shard_map(
        body,
        mesh=mesh,
        in_specs=placed,
        out_specs=(
            P(("groups", "fsdp"), "rows", None, None),
            P(("groups", "fsdp"), "rows", None, None),
            P(("groups", "fsdp", "rows"), None),
            P(("groups", "fsdp", "rows"), None),
        ),
        check_vma=False,
    )
```

profile of v0, /device:TPU:0, one launch (start us, length us, event | category | flops | bytes accessed | tf_op | source)
XLA Modules:
  0.0 278.8 jit_solution(13945911961746731159)
XLA Ops:
  7.2 0.0 copy-start.4
  7.2 0.0 all-gather.3.cloned.1.call-start
  7.2 0.7 all-gather.3.cloned.1.call-update
  7.9 0.0 all-gather.5.cloned.1.call-start
  8.0 0.7 convert_element_type.146
  8.7 6.0 %collective-permute-start.1 = (bf16[1,16,16]{2,1,0:T(8,128)(2,1)S(1)}, bf16[1,16,16]{2,1,0:T(8,128)(2,1)S(1)}, u32[]{:S(2)}, u32[]{:S(2)}) collective-permute-start(bf16[1,16,16]{2,1,0:T(8,128)(2,1)S(1)} %convert_element_type.146), channel_id=1, source_target_pairs={{1,0},{2,1},{3,2},{4,3},{5,4},{6,5},{7,6},{0,7},{9,8},{10,9},{11,1... | collective-permute-start | bytes 1544 | tf_op jit(solution)/shard_map/ppermute | solution.py:14
  14.7 0.5 collective-permute-start.3
  15.2 1.4 collective-permute-start
  16.6 0.0 all-gather.5.cloned.1.call-update
  16.6 0.0 reduce-scatter.5.cloned.1.call-start
  16.7 0.7 convert_bitcast_fusion
  17.4 1.3 fusion.66
  18.7 0.7 compare_convert_fusion
  19.9 0.6 compare_select_fusion.4
  20.6 0.1 broadcast_add_fusion
  23.1 0.1 add.121
  24.5 0.0 collective-permute-done.1
  24.5 0.1 fusion.53
  24.6 0.1 gt.17
  24.7 0.1 fusion.48
  24.9 19.1 %collective-permute-done = bf16[1,16,16,1024]{3,2,1,0:T(8,128)(2,1)S(1)} collective-permute-done((bf16[1,16,16,1024]{3,2,1,0:T(8,128)(2,1)}, bf16[1,16,16,1024]{3,2,1,0:T(8,128)(2,1)S(1)}, u32[]{:S(2)}, u32[]{:S(2)}) %collective-permute-start) | collective-permute-done | bytes 524320 | tf_op jit(solution)/shard_map/ppermute | solution.py:14
  44.0 1.1 fusion.39
  45.1 0.5 convert_reduce_fusion
  45.6 0.0 copy-done.4
  45.6 0.2 fusion.37
  45.8 0.4 fusion.36
  46.2 0.1 div.24
  46.3 0.1 convert_element_type.162
  46.4 0.2 fusion.22
  46.7 0.3 fusion.29
  46.9 22.2 %all-gather.3.cloned.1.call-done = bf16[1024,1536]{1,0:T(8,128)(2,1)} async-done(((bf16[64,1536]{1,0:T(8,128)(2,1)}), bf16[1024,1536]{1,0:T(8,128)(2,1)}) %all-gather.3.cloned.1.call-update) | async-done | bytes 3145744 | tf_op jit(solution)/shard_map/all_gather | solution.py:53
  69.1 3.8 %convolution_convert_fusion = bf16[256,1536]{1,0:T(8,128)(2,1)} fusion(bf16[256,1024]{1,0:T(8,128)(2,1)S(1)} %fusion.29, bf16[1024,1536]{1,0:T(8,128)(2,1)} %all-gather.3.cloned.1.call-done), kind=kOutput, calls=%fused_computation.2 | convolution fusion | flops 805699584 | bytes 4456448 | tf_op jit(solution)/shard_map/dot_general | solution.py:87
  72.9 1.4 copy.21
  74.3 2.2 fusion.67
  76.5 1.9 convolution_convert_fusion.2
  78.4 0.0 copy-start.2
  78.4 0.7 copy-done.2
  79.1 1.8 fusion.68
  80.9 0.0 reduce-scatter.5.cloned.1.call-update
  80.9 0.0 reduce-scatter.3.cloned.1.call-start
  80.9 27.2 %all-gather.5.cloned.1.call-done = bf16[512,1024]{1,0:T(8,128)(2,1)} async-done(((bf16[32,1024]{1,0:T(8,128)(2,1)}), bf16[512,1024]{1,0:T(8,128)(2,1)}) %all-gather.5.cloned.1.call-update) | async-done | bytes 1048592 | tf_op jit(solution)/shard_map/all_gather | solution.py:54
  108.1 1.7 convolution_convert_fusion.1
  109.8 0.1 copy.24
  110.0 1.8 fusion.49
  111.7 4.2 %fusion.14 = bf16[1,256,1,8,64]{1,4,3,2,0:T(8,128)(2,1)S(1)} fusion(f32[8,256,256]{1,2,0:T(8,128)} %fusion.49, bf16[1,256,3,8,64]{1,4,3,2,0:T(8,128)(2,1)S(1)} %bitcast.119, f32[8,256,256]{1,2,0:T(8,128)} %get-tuple-element.11, f32[8,256]{1,0:T(8,128)S(1)} %get-tuple-element.10), kind=kOutput, calls=%fused_computation.15 | convolution fusion | flops 70781184 | bytes 8929280 | tf_op jit(solution)/shard_map/whqk,wkhd->wqhd/dot_general | solution.py:135
  116.0 5.1 %fusion.17 = bf16[1,256,1,8,64]{1,4,3,2,0:T(8,128)(2,1)} fusion(f32[8,256,256]{1,2,0:T(8,128)} %fusion.49, bf16[1,256,3,8,64]{1,4,3,2,0:T(8,128)(2,1)S(1)} %bitcast.120, f32[8,256,256]{1,2,0:T(8,128)} %get-tuple-element.11, f32[8,256]{1,0:T(8,128)S(1)} %get-tuple-element.10), kind=kOutput, calls=%fused_computation.16 | convolution fusion | flops 70781184 | bytes 8929280 | tf_op jit(solution)/shard_map/whqk,wqhd->wkhd/dot_general | solution.py:138
  121.1 2.2 convolution_bitcast_fusion
  123.2 0.1 maximum_convert_fusion
  123.3 3.8 %fusion.31 = f32[1024,1536]{1,0:T(8,128)} fusion(bf16[256,1536]{0,1:T(8,128)(2,1)S(1)} %bitcast.112, f32[1,256,1,1,1,1,1024]{6,1,5,4,3,2,0:T(8,128)S(1)} %bitcast.109, f32[256]{0:T(256)S(1)} %add_rsqrt_fusion, f32[256]{0:T(256)S(1)} %div.24), kind=kOutput, calls=%fused_computation.50 | convolution fusion | flops 806092800 | bytes 8128512 | tf_op jit(solution)/shard_map/dot_general | solution.py:149
  127.2 0.0 reduce-scatter.3.cloned.1.call-update
  128.6 0.3 copy.23
  128.9 0.3 reshape_transpose_reshape_reshape.3
  129.2 3.1 %fusion.64 = (f32[256]{0:T(256)S(1)}, f32[256]{0:T(256)S(1)}, f32[256,1024]{1,0:T(8,128)S(1)}) fusion(f32[256]{0:T(256)S(1)} %add_rsqrt_fusion, f32[256]{0:T(256)S(1)} %div.24, bf16[16,16,1024]{2,1,0:T(8,128)(2,1)S(1)} %get-tuple-element.7, bf16[256,1536]{0,1:T(8,128)(2,1)S(1)} %bitcast.113, bf16[1024,1536]{1,0:T(8,128)(2,1)} %all-gather.3.cloned.1.call-done), kind=kOutput, calls=%fused_computation.106 | convolution fusion | flops 806878720 | bytes 5509120 | tf_op jit(solution)/shard_map/dot_general | solution.py:152
  132.4 0.0 copy-start.1
  132.4 0.4 add_convert_fusion
  132.8 0.4 fusion.35
  133.2 0.5 collective-permute-start.4
  133.7 0.2 fusion.46
  133.9 1.5 collective-permute-start.2
  136.7 27.6 %collective-permute-done.2 = bf16[16,16,512]{2,1,0:T(8,128)(2,1)S(1)} collective-permute-done((bf16[16,16,512]{2,1,0:T(8,128)(2,1)S(1)}, bf16[16,16,512]{2,1,0:T(8,128)(2,1)S(1)}, u32[]{:S(2)}, u32[]{:S(2)}) %collective-permute-start.2) | collective-permute-done | bytes 262176 | tf_op jit(solution)/shard_map/ppermute | solution.py:14
  164.2 1.3 fusion.13
  165.5 1.0 fusion.34
  166.5 16.6 %reduce-scatter.5.cloned.1.call-done = f32[32,1024]{1,0:T(8,128)} async-done(((f32[512,1024]{1,0:T(8,128)}), f32[32,1024]{1,0:T(8,128)}) %reduce-scatter.5.cloned.1.call-update) | async-done | bytes 131088 | tf_op jit(solution)/shard_map/reduce_scatter | solution.py:170
  183.1 89.1 %reduce-scatter.3.cloned.1.call-done = f32[64,1536]{1,0:T(8,128)} async-done(((f32[1024,1536]{1,0:T(8,128)}), f32[64,1536]{1,0:T(8,128)}) %reduce-scatter.3.cloned.1.call-update) | async-done | bytes 393232 | tf_op jit(solution)/shard_map/reduce_scatter | solution.py:169
  (13 shorter events, 0.1 us)
Async XLA Ops:
  7.2 38.4 %copy-start.4 = (bf16[1,16,16,1024]{3,2,1,0:T(8,128)(2,1)S(1)}, bf16[1,16,16,1024]{3,2,1,0:T(8,128)(2,1)}, u32[]{:S(2)}) copy-start(bf16[1,16,16,1024]{3,2,1,0:T(8,128)(2,1)} %param.11) | copy-start | bytes 1572868
  7.2 61.9 %all-gather.3.cloned.1.call-start = ((), (), s32[]{:S(2)}) async-start(), calls=%async_computation.2 | async-start | bytes 3342336 | tf_op jit(solution)/shard_map/all_gather | solution.py:53
  7.9 100.2 %all-gather.5.cloned.1.call-start = ((), (), s32[]{:S(2)}) async-start(), calls=%async_computation.3 | async-start | bytes 1114112 | tf_op jit(solution)/shard_map/all_gather | solution.py:54
  8.7 15.8 %collective-permute-start.1 = (bf16[1,16,16]{2,1,0:T(8,128)(2,1)S(1)}, bf16[1,16,16]{2,1,0:T(8,128)(2,1)S(1)}, u32[]{:S(2)}, u32[]{:S(2)}) collective-permute-start(bf16[1,16,16]{2,1,0:T(8,128)(2,1)S(1)} %convert_element_type.146), channel_id=1, source_target_pairs={{1,0},{2,1},{3,2},{4,3},{5,4},{6,5},{7,6},{0,7},{9,8},{10,9},{11,1... | collective-permute-start | bytes 1544 | tf_op jit(solution)/shard_map/ppermute | solution.py:14
  14.7 30.9 %collective-permute-start.3 = (bf16[1,16,16,1024]{3,2,1,0:T(8,128)(2,1)}, bf16[1,16,16,1024]{3,2,1,0:T(8,128)(2,1)S(1)}, u32[]{:S(2)}, u32[]{:S(2)}) collective-permute-start(bf16[1,16,16,1024]{3,2,1,0:T(8,128)(2,1)} %param.11), channel_id=1, source_target_pairs={{1,0},{2,1},{3,2},{4,3},{5,4},{6,5},{7,6},{0,7},{9,8},{10,9},{11,1... | collective-permute-start | bytes 1572872 | tf_op jit(solution)/shard_map/ppermute | solution.py:14
  15.2 28.8 %collective-permute-start = (bf16[1,16,16,1024]{3,2,1,0:T(8,128)(2,1)}, bf16[1,16,16,1024]{3,2,1,0:T(8,128)(2,1)S(1)}, u32[]{:S(2)}, u32[]{:S(2)}) collective-permute-start(bf16[1,16,16,1024]{3,2,1,0:T(8,128)(2,1)} %param.6), channel_id=1, source_target_pairs={{1,0},{2,1},{3,2},{4,3},{5,4},{6,5},{7,6},{0,7},{9,8},{10,9},{11,1... | collective-permute-start | bytes 1572872 | tf_op jit(solution)/shard_map/ppermute | solution.py:14
  16.6 166.5 %reduce-scatter.5.cloned.1.call-start = ((), (), s32[]{:S(2)}) async-start(), calls=%async_computation.5 | async-start | bytes 2228224 | tf_op jit(solution)/shard_map/reduce_scatter | solution.py:170
  78.4 0.7 copy-start.2
  80.9 191.4 %reduce-scatter.3.cloned.1.call-start = ((), (), s32[]{:S(2)}) async-start(), calls=%async_computation.4 | async-start | bytes 6684672 | tf_op jit(solution)/shard_map/reduce_scatter | solution.py:169
  121.1 2.2 copy-start.5
  127.2 1.4 copy-start.3
  132.4 31.8 %copy-start = (bf16[512,1024]{1,0:T(8,128)(2,1)S(1)}, bf16[512,1024]{1,0:T(8,128)(2,1)}, u32[]{:S(2)}) copy-start(bf16[512,1024]{1,0:T(8,128)(2,1)} %all-gather.5.cloned.1.call-done) | copy-start | bytes 3145732
  132.4 31.8 %copy-start.1 = (bf16[1,16,16,1024]{3,2,1,0:T(8,128)(2,1)S(1)}, bf16[1,16,16,1024]{3,2,1,0:T(8,128)(2,1)}, u32[]{:S(2)}) copy-start(bf16[1,16,16,1024]{3,2,1,0:T(8,128)(2,1)} %param.6) | copy-start | bytes 1572868
  133.2 32.3 %collective-permute-start.4 = (bf16[16,16,1024]{2,1,0:T(8,128)(2,1)S(1)}, bf16[16,16,1024]{2,1,0:T(8,128)(2,1)S(1)}, u32[]{:S(2)}, u32[]{:S(2)}) collective-permute-start(bf16[16,16,1024]{2,1,0:T(8,128)(2,1)S(1)} %fusion.35), channel_id=1, source_target_pairs={{7,0},{0,1},{1,2},{2,3},{3,4},{4,5},{5,6},{6,7},{15,8},{8,9},{9,10... | collective-permute-start | bytes 1572872 | tf_op jit(solution)/shard_map/ppermute | solution.py:14
  133.9 30.3 %collective-permute-start.2 = (bf16[16,16,512]{2,1,0:T(8,128)(2,1)S(1)}, bf16[16,16,512]{2,1,0:T(8,128)(2,1)S(1)}, u32[]{:S(2)}, u32[]{:S(2)}) collective-permute-start(bf16[16,16,512]{2,1,0:T(8,128)(2,1)S(1)} %fusion.46), channel_id=1, source_target_pairs={{7,0},{0,1},{1,2},{2,3},{3,4},{4,5},{5,6},{6,7},{15,8},{8,9},{9,10... | collective-permute-start | bytes 786440 | tf_op jit(solution)/shard_map/ppermute | solution.py:14
Sparse Core Ops, SparseCore 0:
  10.2 58.8 all-gather.2
  71.3 36.7 all-gather.4
  112.4 70.6 reduce-scatter.4
  188.0 84.2 reduce-scatter.2
where the time goes:
time: 279 us
  waiting for transfers between devices  202 us (72%)
  matrix products  32.9 us (12%)
  between operations  20.9 us (7%)
  starting transfers between devices  10.1 us (4%)
  other arithmetic  7.93 us (3%)
  local copies, waits for them, and re-layouts  4.47 us (2%)
    reduce_scatter x1, waiting for transfers between devices, body(): lax.psum_scatter(term_in, ('fsdp', 'rows'), scatter_dimension=0, tiled=True)  89.1 us
    ppermute x5, waiting for transfers between devices, shifted(): return lax.ppermute(block, axis, route)  46.7 us
    all_gather x1, waiting for transfers between devices, body(): lax.all_gather(projection_out, ('fsdp', 'rows'), axis=0, tiled=True)  27.2 us
    all_gather x1, waiting for transfers between devices, body(): lax.all_gather(projection_in, ('fsdp', 'rows'), axis=0, tiled=True)  22.2 us
    reduce_scatter x1, waiting for transfers between devices, body(): lax.psum_scatter(term_out, ('fsdp', 'rows'), scatter_dimension=0, tiled=T...  16.6 us
    ppermute x5, starting transfers between devices, shifted(): return lax.ppermute(block, axis, route)  9.92 us
  transfers between devices with their start and end apart: 9, of which 6 were waited for; matrix products, arithmetic and copies ran while one was open for 16% of the time, Pallas kernels for 0%

commit v1 on v0

--- a/solution.py
+++ b/solution.py
@@ -1,3 +1,4 @@
+import functools
 import jax
 import jax.numpy as jnp
 from jax import lax
@@ -6,6 +7,23 @@
 HEADS = 8
 HD = 64
 WIN = 16
+
+
+def advance_ticks(row_data, group_axis):
+    f_now = lax.psum(1, group_axis)
+    odd = lax.axis_index(group_axis)
+    carry, built = (f_now, odd)
+    extra, formed = (row_data, 1)
+    while formed < carry:
+        ready = lax.ppermute(extra, group_axis, [(no, no ^ formed) for no in range(carry)])
+        y1 = jnp.concatenate([extra, ready], axis=0)
+        high = jnp.concatenate([ready, extra], axis=0)
+        extra = jnp.where(built & formed == 0, y1, high)
+        formed = 2 * formed
+    return extra
+
+
+proceed_object = functools.partial(advance_ticks, group_axis=("fsdp", "rows"))
 
 
 def shifted(block, axis, distance):
@@ -51,7 +69,7 @@
     shift_col = shifts[1]
     full_in, full_out = (
         lax.all_gather(projection_in, ("fsdp", "rows"), axis=0, tiled=True),
-        lax.all_gather(projection_out, ("fsdp", "rows"), axis=0, tiled=True),
+        proceed_object(projection_out),
     )
     mask_wire = cell_mask.astype(jnp.bfloat16)
     next_tokens, next_mask = shifted((tokens, mask_wire), "rows", -1)

time: 279 us -> 238 us (0.85)
  waiting for transfers between devices: 202 us -> 151 us
  starting transfers between devices: 10.1 us -> 13.7 us
  matrix products: 32.9 us -> 36.1 us
  other arithmetic: 7.93 us -> 11.1 us
    all_gather x1 -> x0, waiting for transfers between devices: 27.2 us -> none  [body(): lax.all_gather(projection_out, ('fsdp', 'rows'), axis=0, tiled=True)]
    ppermute x0 -> x4, waiting for transfers between devices: none -> 19.9 us  [advance_ticks(): lax.ppermute(extra, group_axis, [(no, no ^ formed) for no in range(carry)])]
    reduce_scatter x1, waiting for transfers between devices: 16.6 us -> 0.01 us  [body(): lax.psum_scatter(term_out, ('fsdp', 'rows'), scatter_dimension=0, tiled=T...]
    reduce_scatter x1, waiting for transfers between devices: 89.1 us -> 74.3 us  [body(): lax.psum_scatter(term_in, ('fsdp', 'rows'), scatter_dimension=0, tiled=True)]
    ppermute x5, waiting for transfers between devices: 46.7 us -> 33.7 us  [shifted(): return lax.ppermute(block, axis, route)]
    ppermute x0 -> x4, starting transfers between devices: none -> 4.79 us  [advance_ticks(): lax.ppermute(extra, group_axis, [(no, no ^ formed) for no in range(carry)])]
    select_n x0 -> x3, other arithmetic: none -> 3.07 us  [advance_ticks(): extra = jnp.where(built & formed == 0, y1, high)]
  transfers between devices with their start and end apart: 9 -> 12, of which waited for: 6 -> 9; matrix products, arithmetic and copies ran while one was open for 16% -> 17% of each run, Pallas kernels for 0% -> 0%
where the time goes in v1:
time: 238 us
  waiting for transfers between devices  151 us (63%)
  matrix products  36.1 us (15%)
  between operations  21.2 us (9%)
  starting transfers between devices  13.7 us (6%)
  other arithmetic  11.1 us (5%)
  local copies, waits for them, and re-layouts  4.79 us (2%)
    reduce_scatter x1, waiting for transfers between devices, body(): lax.psum_scatter(term_in, ('fsdp', 'rows'), scatter_dimension=0, tiled=True)  74.3 us
    ppermute x5, waiting for transfers between devices, shifted(): return lax.ppermute(block, axis, route)  33.7 us
    all_gather x1, waiting for transfers between devices, body(): lax.all_gather(projection_in, ('fsdp', 'rows'), axis=0, tiled=True)  22.1 us
    ppermute x4, waiting for transfers between devices, advance_ticks(): lax.ppermute(extra, group_axis, [(no, no ^ formed) for no in range(carry)])  19.9 us
    ppermute x5, starting transfers between devices, shifted(): return lax.ppermute(block, axis, route)  8.76 us
    dot_general x1, matrix products, body(): jnp.einsum('whqk,wkhd->wqhd', grad_scores, key_heads, preferred_element_t...  4.99 us
    dot_general x1, matrix products, body(): jnp.einsum('whqk,wqhd->wkhd', grad_scores, query_heads, preferred_element...  4.98 us
    ppermute x4, starting transfers between devices, advance_ticks(): lax.ppermute(extra, group_axis, [(no, no ^ formed) for no in range(carry)])  4.79 us
  transfers between devices with their start and end apart: 12, of which 9 were waited for; matrix products, arithmetic and copies ran while one was open for 17% of the time, Pallas kernels for 0%

profile of v1, /device:TPU:0, one launch (start us, length us, event | category | flops | bytes accessed | tf_op | source)
XLA Modules:
  0.0 237.6 jit_solution(4126988125569818146)
XLA Ops:
  7.2 0.0 all-gather.2.cloned.1.call-start
  7.2 0.7 all-gather.2.cloned.1.call-update
  7.9 0.0 reduce-scatter.5.cloned.1.call-start
  7.9 0.7 convert_element_type.146
  8.6 6.0 %collective-permute-start.1 = (bf16[1,16,16]{2,1,0:T(8,128)(2,1)S(1)}, bf16[1,16,16]{2,1,0:T(8,128)(2,1)S(1)}, u32[]{:S(2)}, u32[]{:S(2)}) collective-permute-start(bf16[1,16,16]{2,1,0:T(8,128)(2,1)S(1)} %convert_element_type.146), channel_id=1, source_target_pairs={{1,0},{2,1},{3,2},{4,3},{5,4},{6,5},{7,6},{0,7},{9,8},{10,9},{11,1... | collective-permute-start | bytes 1544 | tf_op jit(solution)/shard_map/ppermute | solution.py:32
  14.7 0.5 collective-permute-start.7
  15.2 1.4 collective-permute-start
  16.6 1.4 fusion.67
  18.6 0.6 compare_convert_fusion
  19.3 0.7 compare_select_fusion.4
  20.0 0.7 convert_bitcast_fusion
  20.7 0.1 broadcast_add_fusion
  23.4 0.1 add.124
  24.8 0.1 fusion.53
  24.9 0.1 gt.17
  25.0 0.1 fusion.48
  25.1 18.8 %collective-permute-done = bf16[1,16,16,1024]{3,2,1,0:T(8,128)(2,1)S(1)} collective-permute-done((bf16[1,16,16,1024]{3,2,1,0:T(8,128)(2,1)}, bf16[1,16,16,1024]{3,2,1,0:T(8,128)(2,1)S(1)}, u32[]{:S(2)}, u32[]{:S(2)}) %collective-permute-start) | collective-permute-done | bytes 524320 | tf_op jit(solution)/shard_map/ppermute | solution.py:32
  44.0 1.2 fusion.39
  45.1 0.5 convert_reduce_fusion
  45.6 0.1 div.24
  45.7 0.1 convert_element_type.162
  45.8 0.2 fusion.37
  46.1 0.4 fusion.36
  46.5 0.2 fusion.22
  46.7 0.3 fusion.29
  47.0 22.1 %all-gather.2.cloned.1.call-done = bf16[1024,1536]{1,0:T(8,128)(2,1)} async-done(((bf16[64,1536]{1,0:T(8,128)(2,1)}), bf16[1024,1536]{1,0:T(8,128)(2,1)}) %all-gather.2.cloned.1.call-update) | async-done | bytes 3145744 | tf_op jit(solution)/shard_map/all_gather | solution.py:71
  69.1 3.7 %convolution_convert_fusion = bf16[256,1536]{1,0:T(8,128)(2,1)} fusion(bf16[256,1024]{1,0:T(8,128)(2,1)S(1)} %fusion.29, bf16[1024,1536]{1,0:T(8,128)(2,1)} %all-gather.2.cloned.1.call-done), kind=kOutput, calls=%fused_computation.2 | convolution fusion | flops 805699584 | bytes 4456448 | tf_op jit(solution)/shard_map/dot_general | solution.py:105
  72.8 1.4 copy.21
  74.2 2.2 fusion.68
  76.4 1.9 convolution_convert_fusion.2
  78.4 1.8 fusion.69
  80.1 0.0 reduce-scatter.5.cloned.1.call-update
  80.1 0.0 reduce-scatter.3.cloned.1.call-start
  80.2 0.6 collective-permute-start.3
  80.8 3.7 %collective-permute-done.3 = bf16[32,1024]{1,0:T(8,128)(2,1)S(1)} collective-permute-done((bf16[32,1024]{1,0:T(8,128)(2,1)S(1)}, bf16[32,1024]{1,0:T(8,128)(2,1)S(1)}, u32[]{:S(2)}, u32[]{:S(2)}) %collective-permute-start.3) | collective-permute-done | bytes 65568 | tf_op jit(solution)/shard_map/ppermute | solution.py:18
  84.6 2.0 collective-permute-start.4
  86.5 3.2 %collective-permute-done.4 = bf16[64,1024]{1,0:T(8,128)(2,1)} collective-permute-done((bf16[64,1024]{1,0:T(8,128)(2,1)S(1)}, bf16[64,1024]{1,0:T(8,128)(2,1)}, u32[]{:S(2)}, u32[]{:S(2)}) %collective-permute-start.4) | collective-permute-done | bytes 131104 | tf_op jit(solution)/shard_map/ppermute | solution.py:18
  89.7 1.0 maximum_select_fusion.2
  90.8 2.2 collective-permute-start.5
  93.0 10.8 %collective-permute-done.5 = bf16[128,1024]{1,0:T(8,128)(2,1)} collective-permute-done((bf16[128,1024]{1,0:T(8,128)(2,1)S(1)}, bf16[128,1024]{1,0:T(8,128)(2,1)}, u32[]{:S(2)}, u32[]{:S(2)}) %collective-permute-start.5) | collective-permute-done | bytes 262176 | tf_op jit(solution)/shard_map/ppermute | solution.py:18
  103.8 2.0 maximum_select_fusion.1
  105.8 2.2 collective-permute-done.6
  108.0 2.8 %convolution_convert_fusion.1 = bf16[256,512]{1,0:T(8,128)(2,1)} fusion(bf16[256,1024]{1,0:T(8,128)(2,1)S(1)} %bitcast.110, bf16[256,1024]{1,0:T(8,128)(2,1)} %collective-permute-done.6, bf16[256,1024]{1,0:T(8,128)(2,1)} %maximum_select_fusion.1, pred[]{:T(512)S(6)} %eq.46), kind=kOutput, calls=%fused_computation.18 | convolution fusion | flops 273285120 | bytes 1835009 | tf_op jit(solution)/shard_map/dot_general | solution.py:138
  110.8 1.1 copy.24
  111.9 1.8 fusion.49
  113.7 5.0 %fusion.14 = bf16[1,256,1,8,64]{1,4,3,2,0:T(8,128)(2,1)} fusion(f32[8,256,256]{1,2,0:T(8,128)} %fusion.49, bf16[1,256,3,8,64]{1,4,3,2,0:T(8,128)(2,1)S(1)} %bitcast.117, f32[8,256,256]{1,2,0:T(8,128)} %get-tuple-element.11, f32[8,256]{1,0:T(8,128)S(1)} %get-tuple-element.10), kind=kOutput, calls=%fused_computation.15 | convolution fusion | flops 70781184 | bytes 8929280 | tf_op jit(solution)/shard_map/whqk,wkhd->wqhd/dot_general | solution.py:153
  118.7 5.0 %fusion.17 = bf16[1,256,1,8,64]{1,4,3,2,0:T(8,128)(2,1)} fusion(f32[8,256,256]{1,2,0:T(8,128)} %fusion.49, bf16[1,256,3,8,64]{1,4,3,2,0:T(8,128)(2,1)S(1)} %bitcast.118, f32[8,256,256]{1,2,0:T(8,128)} %get-tuple-element.11, f32[8,256]{1,0:T(8,128)S(1)} %get-tuple-element.10), kind=kOutput, calls=%fused_computation.16 | convolution fusion | flops 70781184 | bytes 8929280 | tf_op jit(solution)/shard_map/whqk,wqhd->wkhd/dot_general | solution.py:156
  123.6 2.1 convolution_bitcast_fusion
  125.8 0.1 maximum_convert_fusion
  125.9 3.8 %fusion.31 = f32[1024,1536]{1,0:T(8,128)} fusion(bf16[256,1536]{0,1:T(8,128)(2,1)S(1)} %bitcast.111, f32[1,256,1,1,1,1,1024]{6,1,5,4,3,2,0:T(8,128)S(1)} %bitcast.108, f32[256]{0:T(256)S(1)} %add_rsqrt_fusion, f32[256]{0:T(256)S(1)} %div.24), kind=kOutput, calls=%fused_computation.51 | convolution fusion | flops 806092800 | bytes 8128512 | tf_op jit(solution)/shard_map/dot_general | solution.py:167
  129.7 0.0 reduce-scatter.3.cloned.1.call-update
  131.0 0.3 copy.23
  131.3 0.3 reshape_transpose_reshape_reshape.3
  131.7 0.2 fusion.46
  131.9 0.8 collective-permute-start.2
  132.6 3.1 %fusion.65 = (f32[256]{0:T(256)S(1)}, f32[256]{0:T(256)S(1)}, f32[256,1024]{1,0:T(8,128)S(1)}) fusion(f32[256]{0:T(256)S(1)} %add_rsqrt_fusion, f32[256]{0:T(256)S(1)} %div.24, bf16[16,16,1024]{2,1,0:T(8,128)(2,1)S(1)} %get-tuple-element.7, bf16[256,1536]{0,1:T(8,128)(2,1)S(1)} %bitcast.112, bf16[1024,1536]{1,0:T(8,128)(2,1)} %all-gather.2.cloned.1.call-done), kind=kOutput, calls=%fused_computation.111 | convolution fusion | flops 806878720 | bytes 5509120 | tf_op jit(solution)/shard_map/dot_general | solution.py:170
  135.8 0.4 add_convert_fusion
  136.2 0.4 fusion.35
  136.6 0.1 collective-permute-start.8
  138.0 7.1 %collective-permute-done.2 = bf16[16,16,512]{2,1,0:T(8,128)(2,1)S(1)} collective-permute-done((bf16[16,16,512]{2,1,0:T(8,128)(2,1)S(1)}, bf16[16,16,512]{2,1,0:T(8,128)(2,1)S(1)}, u32[]{:S(2)}, u32[]{:S(2)}) %collective-permute-start.2) | collective-permute-done | bytes 262176 | tf_op jit(solution)/shard_map/ppermute | solution.py:32
  145.1 2.9 %fusion.13 = bf16[1,16,16,1024]{3,2,1,0:T(8,128)(2,1)} fusion(s32[]{:T(128)S(6)} %select_n.80, bf16[16,16,512]{2,1,0:T(8,128)(2,1)S(1)} %collective-permute-done.2, bf16[16,16,512]{2,1,0:T(8,128)(2,1)S(1)} %fusion.46, bf16[256,1024]{1,0:T(8,128)(2,1)} %collective-permute-done.6, bf16[256,1024]{1,0:T(8,128)(2,1)} %maximum_select_fusion.1, pred[]{:T(512)S(6)} %eq.46, ...), kind=kOutput, calls=%fused_computation.14 | convolution fusion | flops 274071552 | bytes 2621445 | tf_op jit(solution)/shard_map/dot_general | solution.py:128
  148.0 7.8 %collective-permute-done.8 = bf16[16,16,1024]{2,1,0:T(8,128)(2,1)S(1)} collective-permute-done((bf16[16,16,1024]{2,1,0:T(8,128)(2,1)S(1)}, bf16[16,16,1024]{2,1,0:T(8,128)(2,1)S(1)}, u32[]{:S(2)}, u32[]{:S(2)}) %collective-permute-start.8) | collective-permute-done | bytes 524320 | tf_op jit(solution)/shard_map/ppermute | solution.py:32
  155.8 1.0 fusion.34
  156.8 74.3 %reduce-scatter.3.cloned.1.call-done = f32[64,1536]{1,0:T(8,128)} async-done(((f32[1024,1536]{1,0:T(8,128)}), f32[64,1536]{1,0:T(8,128)}) %reduce-scatter.3.cloned.1.call-update) | async-done | bytes 393232 | tf_op jit(solution)/shard_map/reduce_scatter | solution.py:187
  (19 shorter events, 0.1 us)
Async XLA Ops:
  7.2 61.9 %all-gather.2.cloned.1.call-start = ((), (), s32[]{:S(2)}) async-start(), calls=%async_computation.2 | async-start | bytes 3342336 | tf_op jit(solution)/shard_map/all_gather | solution.py:71
  7.9 148.9 %reduce-scatter.5.cloned.1.call-start = ((), (), s32[]{:S(2)}) async-start(), calls=%async_computation.4 | async-start | bytes 2228224 | tf_op jit(solution)/shard_map/reduce_scatter | solution.py:188
  8.6 16.1 %collective-permute-start.1 = (bf16[1,16,16]{2,1,0:T(8,128)(2,1)S(1)}, bf16[1,16,16]{2,1,0:T(8,128)(2,1)S(1)}, u32[]{:S(2)}, u32[]{:S(2)}) collective-permute-start(bf16[1,16,16]{2,1,0:T(8,128)(2,1)S(1)} %convert_element_type.146), channel_id=1, source_target_pairs={{1,0},{2,1},{3,2},{4,3},{5,4},{6,5},{7,6},{0,7},{9,8},{10,9},{11,1... | collective-permute-start | bytes 1544 | tf_op jit(solution)/shard_map/ppermute | solution.py:32
  14.7 31.2 %collective-permute-start.7 = (bf16[1,16,16,1024]{3,2,1,0:T(8,128)(2,1)}, bf16[1,16,16,1024]{3,2,1,0:T(8,128)(2,1)S(1)}, u32[]{:S(2)}, u32[]{:S(2)}) collective-permute-start(bf16[1,16,16,1024]{3,2,1,0:T(8,128)(2,1)} %param.11), channel_id=1, source_target_pairs={{1,0},{2,1},{3,2},{4,3},{5,4},{6,5},{7,6},{0,7},{9,8},{10,9},{11,1... | collective-permute-start | bytes 1572872 | tf_op jit(solution)/shard_map/ppermute | solution.py:32
  15.2 28.8 %collective-permute-start = (bf16[1,16,16,1024]{3,2,1,0:T(8,128)(2,1)}, bf16[1,16,16,1024]{3,2,1,0:T(8,128)(2,1)S(1)}, u32[]{:S(2)}, u32[]{:S(2)}) collective-permute-start(bf16[1,16,16,1024]{3,2,1,0:T(8,128)(2,1)} %param.6), channel_id=1, source_target_pairs={{1,0},{2,1},{3,2},{4,3},{5,4},{6,5},{7,6},{0,7},{9,8},{10,9},{11,1... | collective-permute-start | bytes 1572872 | tf_op jit(solution)/shard_map/ppermute | solution.py:32
  44.0 1.9 copy-start
  78.4 1.8 copy-start.4
  80.1 150.9 %reduce-scatter.3.cloned.1.call-start = ((), (), s32[]{:S(2)}) async-start(), calls=%async_computation.3 | async-start | bytes 6684672 | tf_op jit(solution)/shard_map/reduce_scatter | solution.py:187
  80.2 4.3 %collective-permute-start.3 = (bf16[32,1024]{1,0:T(8,128)(2,1)S(1)}, bf16[32,1024]{1,0:T(8,128)(2,1)S(1)}, u32[]{:S(2)}, u32[]{:S(2)}) collective-permute-start(bf16[32,1024]{1,0:T(8,128)(2,1)S(1)} %copy-done.4), channel_id=1, source_target_pairs={{0,1},{1,0},{2,3},{3,2},{4,5},{5,4},{6,7},{7,6},{8,9},{9,8},{10,11... | collective-permute-start | bytes 196616 | tf_op jit(solution)/shard_map/ppermute | solution.py:18
  84.6 5.1 %collective-permute-start.4 = (bf16[64,1024]{1,0:T(8,128)(2,1)S(1)}, bf16[64,1024]{1,0:T(8,128)(2,1)}, u32[]{:S(2)}, u32[]{:S(2)}) collective-permute-start(bf16[64,1024]{1,0:T(8,128)(2,1)S(1)} %maximum_select_fusion.5), channel_id=1, source_target_pairs={{0,2},{1,3},{2,0},{3,1},{4,6},{5,7},{6,4},{7,5},{8,10},{9,11},{10,... | collective-permute-start | bytes 393224 | tf_op jit(solution)/shard_map/ppermute | solution.py:18
  90.8 13.0 %collective-permute-start.5 = (bf16[128,1024]{1,0:T(8,128)(2,1)S(1)}, bf16[128,1024]{1,0:T(8,128)(2,1)}, u32[]{:S(2)}, u32[]{:S(2)}) collective-permute-start(bf16[128,1024]{1,0:T(8,128)(2,1)S(1)} %maximum_select_fusion.2), channel_id=1, source_target_pairs={{0,4},{1,5},{2,6},{3,7},{4,0},{5,1},{6,2},{7,3},{8,12},{9,13},{10,... | collective-permute-start | bytes 786440 | tf_op jit(solution)/shard_map/ppermute | solution.py:18
  105.8 2.3 collective-permute-start.6
  123.6 2.1 copy-start.2
  123.6 2.1 copy-start.3
  131.9 13.3 %collective-permute-start.2 = (bf16[16,16,512]{2,1,0:T(8,128)(2,1)S(1)}, bf16[16,16,512]{2,1,0:T(8,128)(2,1)S(1)}, u32[]{:S(2)}, u32[]{:S(2)}) collective-permute-start(bf16[16,16,512]{2,1,0:T(8,128)(2,1)S(1)} %fusion.46), channel_id=1, source_target_pairs={{7,0},{0,1},{1,2},{2,3},{3,4},{4,5},{5,6},{6,7},{15,8},{8,9},{9,10... | collective-permute-start | bytes 786440 | tf_op jit(solution)/shard_map/ppermute | solution.py:32
  135.8 9.4 %copy-start.1 = (bf16[1,16,16,1024]{3,2,1,0:T(8,128)(2,1)S(1)}, bf16[1,16,16,1024]{3,2,1,0:T(8,128)(2,1)}, u32[]{:S(2)}) copy-start(bf16[1,16,16,1024]{3,2,1,0:T(8,128)(2,1)} %param.6) | copy-start | bytes 1572868
  136.6 19.2 %collective-permute-start.8 = (bf16[16,16,1024]{2,1,0:T(8,128)(2,1)S(1)}, bf16[16,16,1024]{2,1,0:T(8,128)(2,1)S(1)}, u32[]{:S(2)}, u32[]{:S(2)}) collective-permute-start(bf16[16,16,1024]{2,1,0:T(8,128)(2,1)S(1)} %fusion.35), channel_id=1, source_target_pairs={{7,0},{0,1},{1,2},{2,3},{3,4},{4,5},{5,6},{6,7},{15,8},{8,9},{9,10... | collective-permute-start | bytes 1572872 | tf_op jit(solution)/shard_map/ppermute | solution.py:32
Sparse Core Ops, SparseCore 0:
  10.2 58.8 all-gather.1
  80.3 60.4 reduce-scatter.4
  145.8 85.2 reduce-scatter.2
